TPU v7x, 256 devices: a whole 4x4x8 slice. The times are simulated.
256 devices in a mesh: row: 32 (over y, x, z_hi), col: 8 (over z_lo, core).
Axes of the slice: x: 4, y: 4, z: 8 (z_hi: 2, z_lo: 4; z = z_hi * 4 + z_lo), core: 2. Of those that a mesh axis runs over, the one named last changes fastest.
Arguments:
- green_function: float32 [64, 64, 64, 128], P('row', 'col'), may hold values from -3 to 3
- hamiltonian: float32 [64, 128], replicated, may hold values from -3 to 3
Outputs:
- green_out: float32 [64, 64, 64, 128], P('row', 'col')
All inputs are finite; a program needn't handle non-finite values.
Results may differ from a plain program's by a relative error of at most 0.00019.
Values sent between devices are 32-bit elements; how exact they have to be, the bound alone decides.
No kernel may reach another device: no remote copies, remote signals or barrier semaphores. Data moves between devices by JAX's collectives and lax.ppermute only.
A program may use at most 64 MiB of HBM per device.

v0:
```python
import jax
import jax.numpy as jnp
from jax import lax
from jax.sharding import PartitionSpec as P

STEPS = 2


time_step = 0.1


def rotate(values):
    half = values.shape[-1] // 2
    return jnp.concatenate([-values[..., half:], values[..., :half]], axis=-1)


def body(green_function, hamiltonian):
    local_rows = green_function.shape[0]
    local_cols = green_function.shape[1]
    orbits = green_function.shape[2]
    row_first = lax.axis_index("row") * local_rows
    col_first = lax.axis_index("col") * local_cols
    first = row_first + jnp.arange(local_rows, dtype=jnp.int32)[:, None]
    second = col_first + jnp.arange(local_cols, dtype=jnp.int32)[None, :]
    weight = jnp.where(
        second < first,
        jnp.float32(1.0),
        jnp.where(second == first, jnp.float32(0.5), jnp.float32(0.0)),
    )
    ham_real = hamiltonian[:, :orbits]
    ham_imag = hamiltonian[:, orbits:]
    for repeat in range(STEPS):
        real_part = green_function[..., :orbits]
        imag_part = green_function[..., orbits:]
        magnitude = real_part * real_part + imag_part * imag_part
        scaled = jnp.concatenate([magnitude, magnitude], axis=-1) * green_function
        sigma = -(time_step * weight)[:, :, None, None] * scaled
        sigma_pair = jnp.concatenate([-sigma, rotate(sigma)], axis=2)
        gathered = lax.all_gather(green_function, "row", axis=0, tiled=True)
        partial_value = jnp.einsum(
            "tsxq,uskq->tukx", sigma_pair, gathered, precision=lax.Precision.HIGHEST
        )
        owned = lax.psum_scatter(partial_value, "col", scatter_dimension=1, tiled=True)
        integral = (
            owned.reshape(local_rows, local_cols, orbits, 2, orbits)
            .transpose(0, 1, 4, 3, 2)
            .reshape(local_rows, local_cols, orbits, 2 * orbits)
        )
        driven = jnp.einsum(
            "ij,tujq->tuiq", ham_real, green_function, precision=lax.Precision.HIGHEST
        )
        driven = driven + jnp.einsum(
            "ij,tujq->tuiq", ham_imag, rotate(green_function), precision=lax.Precision.HIGHEST
        )
        driven = driven + integral
        green_function = green_function - time_step * rotate(driven)
    return green_function


def solution(mesh):
    in_specs = (P("row", "col", None, None), P())
    out_specs = P("row", "col", None, None)
    return jax.shard_map(body, mesh=mesh, in_specs=in_specs, out_specs=out_specs, check_vma=False)
```

profile of v0, /device:TPU:2, one launch (start us, length us, event | category | flops | bytes accessed | tf_op | source)
XLA Modules:
  0.0 665.4 jit_solution(9457979344891670571)
XLA Ops:
  6.5 0.7 all-gather.3.cloned.1.call-update
  7.3 0.1 fusion.43
  7.4 2.2 slice_negate_fusion.5
  9.6 1.3 fusion.50
  10.9 0.2 slice_negate_fusion.3
  11.1 248.5 %all-gather.3.cloned.1.call-done = f32[64,8,64,128]{3,2,1,0:T(8,128)} async-done(((f32[2,8,64,128]{3,2,1,0:T(8,128)}), f32[64,8,64,128]{3,2,1,0:T(8,128)}) %all-gather.3.cloned.1.call-update) | async-done | bytes 16777232 | tf_op jit(solution)/shard_map/all_gather | solution.py:39
  259.6 18.0 %fusion.4 = f32[2,64,64,128]{3,2,1,0:T(8,128)S(1)} fusion(f32[64,8,64,128]{3,2,1,0:T(8,128)} %all-gather.3.cloned.1.call-done, f32[2,8,64,64]{3,2,1,0:T(8,128)S(1)} %get-tuple-element.22, f32[2,8,64,64]{3,2,1,0:T(8,128)S(1)} %get-tuple-element.21, f32[2,8,64,128]{3,2,1,0:T(8,128)S(1)} %get-tuple-element.7), kind=kOutput, calls=%fused_computation.5 | convolution fusion | flops 12885426176 | bytes 22020096 | tf_op jit(solution)/shard_map/tsxq,uskq->tukx/dot_general | solution.py:40
  277.6 0.6 copy.13
  278.2 4.3 copy.20
  282.6 1.4 fusion.36
  284.0 48.5 %reduce-scatter.8.cloned.1.call-done = f32[8,16384]{1,0:T(8,128)} async-done(((f32[64,16384]{1,0:T(8,128)}), f32[8,16384]{1,0:T(8,128)}) %reduce-scatter.8.cloned.1.call-update) | async-done | bytes 524304
  332.5 1.1 copy.18
  333.7 0.6 reshape.95
  334.3 1.5 copy.5
  335.8 0.6 reshape.82
  336.4 1.9 fusion.13
  338.3 0.2 slice_negate_fusion.2
  338.5 1.0 fusion.26
  339.6 0.2 reduce-scatter.6.cloned.1.call-start
  339.8 2.2 slice_negate_fusion.4
  342.0 1.3 fusion.48
  343.3 0.2 slice_negate_fusion.1
  343.5 241.0 %all-gather.5.cloned.1.call-done = f32[64,8,64,128]{3,2,1,0:T(8,128)} async-done(((f32[2,8,64,128]{3,2,1,0:T(8,128)}), f32[64,8,64,128]{3,2,1,0:T(8,128)}) %all-gather.5.cloned.1.call-update) | async-done | bytes 16777232 | tf_op jit(solution)/shard_map/all_gather | solution.py:39
  584.5 17.5 %fusion.7 = f32[2,64,64,128]{3,2,0,1:T(8,128)} fusion(f32[64,8,64,128]{3,2,1,0:T(8,128)} %all-gather.5.cloned.1.call-done, f32[2,8,64,64]{3,2,1,0:T(8,128)S(1)} %get-tuple-element.15, f32[2,8,64,64]{3,2,1,0:T(8,128)S(1)} %get-tuple-element.14, f32[2,8,64,128]{3,2,1,0:T(8,128)S(1)} %get-tuple-element.5), kind=kOutput, calls=%fused_computation.6 | convolution fusion | flops 12885426176 | bytes 22020096 | tf_op jit(solution)/shard_map/tsxq,uskq->tukx/dot_general | solution.py:40
  602.0 1.4 fusion.34
  603.4 48.6 %reduce-scatter.6.cloned.1.call-done = f32[2,8,64,128]{3,2,0,1:T(8,128)} async-done(((f32[2,64,64,128]{3,2,0,1:T(8,128)}), f32[2,8,64,128]{3,2,0,1:T(8,128)}) %reduce-scatter.6.cloned.1.call-update) | async-done | bytes 524304 | tf_op jit(solution)/shard_map/reduce_scatter | solution.py:43
  652.0 1.6 reshape.83
  653.7 1.5 copy.6
  655.2 0.6 reshape.84
  655.7 1.9 fusion.11
  657.7 0.2 slice_negate_fusion
  657.9 1.0 fusion.31
  (14 shorter events, 0.2 us)
Async XLA Ops:
  6.5 253.1 %all-gather.3.cloned.1.call-start = ((), (), s32[]{:S(2)}) async-start(), calls=%async_computation.2 | async-start | bytes 17301504 | tf_op jit(solution)/shard_map/all_gather | solution.py:39
  7.3 325.3 %reduce-scatter.8.cloned.1.call-start = ((), (), s32[]{:S(2)}) async-start(), calls=%async_computation.5 | async-start | bytes 4718592
  259.6 23.0 %copy-start.1 = (f32[2,8,64,128]{3,2,1,0:T(8,128)S(1)}, f32[2,8,64,128]{3,2,1,0:T(8,128)}, u32[]{:S(2)}) copy-start(f32[2,8,64,128]{3,2,1,0:T(8,128)} %param.2) | copy-start | bytes 1572868
  259.6 23.0 %copy-start.2 = (f32[64,128]{1,0:T(8,128)S(1)}, f32[64,128]{1,0:T(8,128)}, u32[]{:S(2)}) copy-start(f32[64,128]{1,0:T(8,128)} %param.3) | copy-start | bytes 98308
  282.6 302.0 %all-gather.5.cloned.1.call-start = ((), (), s32[]{:S(2)}) async-start(), calls=%async_computation.3 | async-start | bytes 17301504 | tf_op jit(solution)/shard_map/all_gather | solution.py:39
  339.6 312.4 %reduce-scatter.6.cloned.1.call-start = ((), (), s32[]{:S(2)}) async-start(), calls=%async_computation.4 | async-start | bytes 4718592 | tf_op jit(solution)/shard_map/reduce_scatter | solution.py:43
  584.5 17.5 %copy-start = (f32[2,8,64,128]{3,2,1,0:T(8,128)S(1)}, f32[2,8,64,128]{3,2,1,0:T(8,128)}, u32[]{:S(2)}) copy-start(f32[2,8,64,128]{3,2,1,0:T(8,128)} %fusion.26) | copy-start | bytes 1572868
Sparse Core Ops, SparseCore 0:
  10.8 248.8 all-gather.2
  282.7 49.8 reduce-scatter.7
  339.7 244.7 all-gather.4
  602.2 49.8 reduce-scatter.5
where the time goes:
time: 666 us; the launch traced here: 665 us
  waiting for transfers between devices  587 us (88%)
  matrix products  42.2 us (6%)
  between operations  13.3 us (2%)
  local copies, waits for them, and re-layouts  12.5 us (2%)
  other arithmetic  9.84 us (1%)
    all_gather x2, waiting for transfers between devices, body(): gathered = lax.all_gather(green_function, 'row', axis=0, tiled=True)  490 us
    unnamed x5, waiting for transfers between devices  49.2 us
    reduce_scatter x1, waiting for transfers between devices, body(): lax.psum_scatter(partial_value, 'col', scatter_dimension=1, tiled=True)  48.6 us
    dot_general x2, matrix products, body(): jnp.einsum('tsxq,uskq->tukx', sigma_pair, gathered, precision=lax.Precisi...  35.5 us
  transfers between devices with their start and end apart: 4, of which 4 were waited for; matrix products, arithmetic and copies ran while one was open for 2% of the time, Pallas kernels for 0%

commit v1 on v0

v1 whole, which is shorter than its diff:
```python
import functools

import jax
import jax.numpy as jnp
from jax import lax
from jax.experimental import pallas as pl
from jax.experimental.pallas import tpu as pltpu
from jax.sharding import Mesh, PartitionSpec as P

STEPS = 2
DT = 0.1
F32, BF16 = jnp.float32, jnp.bfloat16
N = 64
W = 2 * N


def rotate(values):
    lane = lax.broadcasted_iota(jnp.int32, values.shape, values.ndim - 1)
    rolled = pltpu.roll(values, N, values.ndim - 1)
    return jnp.where(lane < N, -rolled, rolled)


def split(values):
    high = values.astype(BF16)
    return high, (values - high.astype(F32)).astype(BF16)


def dot_t(a, b):
    return lax.dot_general(a, b, (((1,), (1,)), ((), ())), preferred_element_type=F32)


def kernel(last, pos, *refs):
    t_refs, own_refs, other_refs = refs[0:4], refs[4:8], refs[8:12]
    ham, out, lhs_hi, lhs_lo, rhs_hi, rhs_lo, stacked = refs[12:]
    y, x, zh, zl, c = (pos[n] for n in range(5))
    zpp = pl.program_id(0)

    def place(value, ypp, j, xp, zp):
        if last:
            out[zp, ypp, xp, 0, j] = value
        else:
            out[0, ypp, j, xp, zp] = value

    @pl.when(zpp == 0)
    def _():
        for k in range(4):
            xp = lax.rem(x - k + 4, 4)
            for zp in range(2):
                t = 16 * y + 4 * xp + 2 * zp + c
                row = (2 * k + zp) * N
                for n in range(8):
                    s = 16 * zl + 4 * (n // 2) + 2 * zh + n % 2
                    weight = jnp.where(s < t, F32(DT * DT), jnp.where(s == t, F32(0.5 * DT * DT), F32(0.0)))
                    g = t_refs[k][zp, n // 2, n % 2]
                    square = g * g
                    scaled = ((square + pltpu.roll(square, N, 1)) * weight) * g
                    high, low = split(scaled)
                    lhs_hi[row:row + N, n * W:(n + 1) * W] = high
                    lhs_lo[row:row + N, n * W:(n + 1) * W] = low

    for k in range(4):
        ypp = lax.rem(y - k + 4, 4)
        for side, ref in ((0, own_refs[k]), (1, other_refs[k])):
            for n in range(8):
                g = ref[0, n // 2, n % 2]
                row = side * W
                col = slice(n * W, (n + 1) * W)
                high, low = split(rotate(g))
                rhs_hi[row:row + N, col] = high
                rhs_lo[row:row + N, col] = low
                high, low = split(-g)
                rhs_hi[row + N:row + W, col] = high
                rhs_lo[row + N:row + W, col] = low
        total = dot_t(lhs_lo[...], rhs_hi[...]) + dot_t(lhs_hi[...], rhs_lo[...]) + dot_t(lhs_hi[...], rhs_hi[...])
        for side in range(2):
            j = c if side == 0 else 1 - c
            for kk in range(4):
                xp = lax.rem(x - kk + 4, 4)
                for zp in range(2):
                    row = (2 * kk + zp) * N
                    place(total[row:row + N, side * W:(side + 1) * W], ypp, j, xp, zp)

    @pl.when(zpp == zh)
    def _():
        for kk in range(4):
            for zp in range(2):
                for j in range(2):
                    n = (2 * kk + zp) * 2 + j
                    g = t_refs[kk][zp, x, j]
                    stacked[:N, n * W:(n + 1) * W] = -rotate(g)
                    stacked[N:, n * W:(n + 1) * W] = g
        turned = DT * lax.dot_general(
            ham[...], stacked[...], (((1,), (0,)), ((), ())),
            preferred_element_type=F32, precision=lax.Precision.HIGHEST,
        )
        for kk in range(4):
            xp = lax.rem(x - kk + 4, 4)
            for zp in range(2):
                for j in range(2):
                    n = (2 * kk + zp) * 2 + j
                    base = stacked[N:, n * W:(n + 1) * W] + turned[:, n * W:(n + 1) * W]
                    if last:
                        out[zp, zl, xp, 0, j] += base
                    else:
                        out[0, zl, j, xp, zp] += base


def partial_sums(last, pos, t_blocks, own_blocks, other_blocks, ham):
    whole = pl.BlockSpec((2, 4, 2, N, W), lambda n, pos: (0, 0, 0, 0, 0))
    half = pl.BlockSpec((1, 4, 2, N, W), lambda n, pos: (n, 0, 0, 0, 0))
    if last:
        shape = (2, 4, 4, 2, 2, N, W)
        out_spec = pl.BlockSpec((2, 4, 4, 1, 2, N, W), lambda n, pos: (0, 0, 0, n, 0, 0, 0))
    else:
        shape = (2, 4, 2, 4, 2, N, W)
        out_spec = pl.BlockSpec((1, 4, 2, 4, 2, N, W), lambda n, pos: (n, 0, 0, 0, 0, 0, 0))
    return pl.pallas_call(
        functools.partial(kernel, last),
        grid_spec=pltpu.PrefetchScalarGridSpec(
            num_scalar_prefetch=1,
            grid=(2,),
            in_specs=[whole] * 4 + [half] * 8 + [pl.BlockSpec((N, W), lambda n, pos: (0, 0))],
            out_specs=out_spec,
            scratch_shapes=[
                pltpu.VMEM((8 * N, 8 * W), BF16),
                pltpu.VMEM((8 * N, 8 * W), BF16),
                pltpu.VMEM((2 * W, 8 * W), BF16),
                pltpu.VMEM((2 * W, 8 * W), BF16),
                pltpu.VMEM((W, 16 * W), F32),
            ],
        ),
        out_shape=jax.ShapeDtypeStruct(shape, F32),
        compiler_params=pltpu.CompilerParams(vmem_limit_bytes=48 * 1024 * 1024),
        name="partial_sums",
    )(pos, *t_blocks, *own_blocks, *other_blocks, ham)


def ring(shift):
    return [(n, (n + shift) % 4) for n in range(4)]


SWAP = [(0, 1), (1, 0)]


def body(green, hamiltonian):
    pos = jnp.stack([lax.axis_index(a) for a in ("y", "x", "zh", "zl", "c")]).astype(jnp.int32)
    block = green.reshape(2, 2, 2, 2, N, W).transpose(2, 0, 1, 3, 4, 5).reshape(4, 2, 2, N, W)
    block = lax.all_to_all(block, ("zh", "c"), 0, 0, tiled=True)
    block = block.reshape(2, 4, 2, N, W)
    for step in range(STEPS):
        last = step == STEPS - 1
        t_blocks = [block] + [lax.ppermute(block, "x", ring(k)) for k in (1, 2, 3)]
        own = [block] + [lax.ppermute(block, "y", ring(k)) for k in (1, 2, 3)]
        other = [lax.ppermute(v, "c", SWAP) for v in own]
        sums = partial_sums(last, pos, t_blocks, own, other, hamiltonian)
        sums = sums.reshape((8,) + sums.shape[2:])
        sums = lax.psum_scatter(sums, ("zh", "zl"), scatter_dimension=0, tiled=True)[0]
        if not last:
            moved = lax.all_to_all(sums.transpose(1, 2, 0, 3, 4), "x", 0, 0, tiled=True)
            block = moved.transpose(1, 0, 2, 3, 4)
        else:
            moved = lax.all_to_all(sums, "x", 0, 0, tiled=True)
            moved = lax.all_to_all(moved.reshape(2, 8, N, W), "c", 0, 0, tiled=True)
    return moved


def solution(mesh):
    fine = Mesh(mesh.devices.reshape(4, 4, 2, 4, 2), ("y", "x", "zh", "zl", "c"))
    spec = P(("y", "x", "zh"), ("zl", "c"), None, None)
    return jax.shard_map(body, mesh=fine, in_specs=(spec, P()), out_specs=spec, check_vma=False)
```

time: 666 us -> 290 us (0.44)
  waiting for transfers between devices: 587 us -> 174 us
  blocking collectives: 0 us -> 51.8 us
  matrix products: 42.2 us -> 0 us
  Pallas kernels: 0 us -> 23.8 us
  starting transfers between devices: 0.31 us -> 16.8 us
  other arithmetic: 9.84 us -> 0 us
    all_gather x2 -> x0, waiting for transfers between devices: 490 us -> none  [body(): gathered = lax.all_gather(green_function, 'row', axis=0, tiled=True)]
    reduce_scatter x1 -> x2, waiting for transfers between devices: 48.6 us -> 112 us  [body(): lax.psum_scatter(sums, ('zh', 'zl'), scatter_dimension=0, tiled=True)[0]]
    ppermute x0 -> x20, waiting for transfers between devices: none -> 62 us  [the longest x6 43.9 us: body(): own = [block] + [lax.ppermute(block, 'y', ring(k)) for k in (1, 2, 3)]]
    all_to_all x0 -> x4, blocking collectives: none -> 51.8 us  [the longest x1 22.2 us: body(): block = lax.all_to_all(block, ('zh', 'c'), 0, 0, tiled=True)]
    unnamed x5 -> x2, waiting for transfers between devices: 49.2 us -> 0.03 us
    dot_general x6 -> x0, matrix products: 42.2 us -> none  [the longest x2 35.5 us: body(): jnp.einsum('tsxq,uskq->tukx', sigma_pair, gathered, precision=lax.Precisi...]
    pallas_call x0 -> x2, Pallas kernels: none -> 23.8 us  [partial_sums(): pl.pallas_call(functools.partial(kernel, last), grid_spec=pltpu.PrefetchS...]
    ppermute x0 -> x20, starting transfers between devices: none -> 16.8 us  [the longest x6 9.13 us: body(): own = [block] + [lax.ppermute(block, 'y', ring(k)) for k in (1, 2, 3)]]
  transfers between devices with their start and end apart: 4 -> 22, of which waited for: 4 -> 8; matrix products, arithmetic and copies ran while one was open for 2% -> 0% of each run, Pallas kernels for 0% -> 0%
where the time goes in v1:
time: 290 us; the launch traced here: 288 us
  waiting for transfers between devices  174 us (60%)
  blocking collectives  51.8 us (18%)
  Pallas kernels  23.8 us (8%)
  starting transfers between devices  16.8 us (6%)
  between operations  13.5 us (5%)
  local copies, waits for them, and re-layouts  7.52 us (3%)
    reduce_scatter x2, waiting for transfers between devices, body(): lax.psum_scatter(sums, ('zh', 'zl'), scatter_dimension=0, tiled=True)[0]  112 us
    ppermute x6, waiting for transfers between devices, body(): own = [block] + [lax.ppermute(block, 'y', ring(k)) for k in (1, 2, 3)]  43.9 us
    pallas_call x2, Pallas kernels, partial_sums(): pl.pallas_call(functools.partial(kernel, last), grid_spec=pltpu.PrefetchS...  23.8 us
    all_to_all x1, blocking collectives, body(): block = lax.all_to_all(block, ('zh', 'c'), 0, 0, tiled=True)  22.2 us
    ppermute x6, waiting for transfers between devices, body(): t_blocks = [block] + [lax.ppermute(block, 'x', ring(k)) for k in (1, 2, 3)]  18.2 us
    all_to_all x1, blocking collectives, body(): moved = lax.all_to_all(sums, 'x', 0, 0, tiled=True)  12.8 us
    all_to_all x1, blocking collectives, body(): moved = lax.all_to_all(sums.transpose(1, 2, 0, 3, 4), 'x', 0, 0, tiled=True)  12.8 us
    ppermute x6, starting transfers between devices, body(): own = [block] + [lax.ppermute(block, 'y', ring(k)) for k in (1, 2, 3)]  9.13 us
  transfers between devices with their start and end apart: 22, of which 8 were waited for; matrix products, arithmetic and copies ran while one was open for 0% of the time, Pallas kernels for 0%

profile of v1, /device:TPU:2, one launch (start us, length us, event | category | flops | bytes accessed | tf_op | source)
XLA Modules:
  0.0 287.8 jit_solution(14911744747403004875)
XLA Ops:
  6.5 1.1 copy.5
  7.6 22.2 %all_to_all.20 = f32[4,2,2,64,128]{4,3,2,1,0:T(8,128)S(1)} all-to-all(f32[4,2,2,64,128]{4,3,2,1,0:T(8,128)S(1)} %bitcast.41), channel_id=1, replica_groups=mesh['y'=4,'x'=4,'zh'=2,'zl'=4,'c'=2] {'zh','c'}, dimensions={0} | all-to-all | bytes 1048576 | tf_op jit(solution)/shard_map/all_to_all | solution.py:148
  29.8 3.0 %collective-permute-start.5 = (f32[2,4,2,64,128]{4,3,2,1,0:T(8,128)S(1)}, f32[2,4,2,64,128]{4,3,2,1,0:T(8,128)S(1)}, u32[]{:S(2)}, u32[]{:S(2)}) collective-permute-start(f32[2,4,2,64,128]{4,3,2,1,0:T(8,128)S(1)} %bitcast.21), channel_id=1, source_target_pairs={{0,192},{64,0},{128,64},{192,128},{1,193},{65,1},{129,65},{193,129... | collective-permute-start | bytes 1572872 | tf_op jit(solution)/shard_map/ppermute | solution.py:153
  32.8 0.6 collective-permute-start.4
  33.4 1.0 collective-permute-start.3
  34.4 0.5 collective-permute-start.2
  34.9 2.4 collective-permute-start.1
  37.4 18.5 %collective-permute-done.5.refs_7_ = f32[2,4,2,64,128]{4,3,2,1,0:T(8,128)S(1)} collective-permute-done((f32[2,4,2,64,128]{4,3,2,1,0:T(8,128)S(1)}, f32[2,4,2,64,128]{4,3,2,1,0:T(8,128)S(1)}, u32[]{:S(2)}, u32[]{:S(2)}) %collective-permute-start.5) | collective-permute-done | bytes 524320 | tf_op jit(solution)/shard_map/ppermute | solution.py:153
  55.9 1.5 collective-permute-start
  57.4 2.2 collective-permute-done.3.refs_5_
  59.6 0.5 collective-permute-start.7
  60.2 9.1 %collective-permute-done.refs_1_ = f32[2,4,2,64,128]{4,3,2,1,0:T(8,128)} collective-permute-done((f32[2,4,2,64,128]{4,3,2,1,0:T(8,128)S(1)}, f32[2,4,2,64,128]{4,3,2,1,0:T(8,128)}, u32[]{:S(2)}, u32[]{:S(2)}) %collective-permute-start) | collective-permute-done | bytes 524320 | tf_op jit(solution)/shard_map/ppermute | solution.py:152
  69.3 0.7 copy-done
  70.1 12.6 %partial_sums.2 = f32[2,4,2,4,2,64,128]{6,5,4,3,2,1,0:T(8,128)} custom-call(s32[5]{0:T(128)S(1)} %stack.23.pos, f32[2,4,2,64,128]{4,3,2,1,0:T(8,128)S(1)} %bitcast.27, f32[2,4,2,64,128]{4,3,2,1,0:T(8,128)} %collective-permute-done.refs_1_, f32[2,4,2,64,128]{4,3,2,1,0:T(8,128)} %collective-permute-done.1.refs_2_, ...), custom_call_target="tpu_custom_call" | custom-call | tf_op jit(solution)/shard_map/partial_sums/pallas_call | solution.py:117
  82.7 4.8 %copy.6 = f32[8,2,4,2,64,128]{5,4,1,3,2,0:T(8,128)} copy(f32[8,2,4,2,64,128]{5,4,3,2,1,0:T(8,128)} %bitcast.39) | data formatting | bytes 8388608 | tf_op jit(solution)/shard_map/reshape | solution.py:156
  87.5 57.7 %reduce-scatter.3.cloned.1.call-done = f32[1,2,4,2,64,128]{5,4,1,3,2,0:T(8,128)} async-done(((f32[8,2,4,2,64,128]{5,4,1,3,2,0:T(8,128)}), f32[1,2,4,2,64,128]{5,4,1,3,2,0:T(8,128)}) %reduce-scatter.3.cloned.1.call-update) | async-done | bytes 524304 | tf_op jit(solution)/shard_map/reduce_scatter | solution.py:157
  145.2 12.8 %all_to_all.21 = f32[4,2,2,64,128]{4,3,2,1,0:T(8,128)S(1)} all-to-all(f32[4,2,2,64,128]{4,3,2,1,0:T(8,128)} %bitcast.43), channel_id=1, replica_groups=mesh['y'=4,'x'=4,'zh'=2,'zl'=4,'c'=2] {'x'}, dimensions={0} | all-to-all | bytes 1048576 | tf_op jit(solution)/shard_map/all_to_all | solution.py:159
  158.0 0.3 collective-permute-start.16
  158.3 2.8 collective-permute-start.15
  161.1 0.8 collective-permute-start.14
  162.0 0.9 collective-permute-start.13
  162.8 1.5 collective-permute-start.12
  164.3 0.2 collective-permute-start.11
  164.5 19.7 %collective-permute-done.15.refs_7_ = f32[2,4,2,64,128]{4,3,2,1,0:T(8,128)S(1)} collective-permute-done((f32[2,4,2,64,128]{4,3,2,1,0:T(8,128)S(1)}, f32[2,4,2,64,128]{4,3,2,1,0:T(8,128)S(1)}, u32[]{:S(2)}, u32[]{:S(2)}) %collective-permute-start.15) | collective-permute-done | bytes 524320 | tf_op jit(solution)/shard_map/ppermute | solution.py:153
  184.4 3.5 %collective-permute-done.13.refs_5_ = f32[2,4,2,64,128]{4,3,2,1,0:T(8,128)S(1)} collective-permute-done((f32[2,4,2,64,128]{4,3,2,1,0:T(8,128)S(1)}, f32[2,4,2,64,128]{4,3,2,1,0:T(8,128)S(1)}, u32[]{:S(2)}, u32[]{:S(2)}) %collective-permute-start.13) | collective-permute-done | bytes 524320 | tf_op jit(solution)/shard_map/ppermute | solution.py:153
  187.9 0.5 collective-permute-start.17
  188.4 9.0 %collective-permute-done.10.refs_1_ = f32[2,4,2,64,128]{4,3,2,1,0:T(8,128)S(1)} collective-permute-done((f32[2,4,2,64,128]{4,3,2,1,0:T(8,128)S(1)}, f32[2,4,2,64,128]{4,3,2,1,0:T(8,128)S(1)}, u32[]{:S(2)}, u32[]{:S(2)}) %collective-permute-start.10) | collective-permute-done | bytes 524320 | tf_op jit(solution)/shard_map/ppermute | solution.py:152
  197.4 11.2 %partial_sums.3 = f32[2,4,4,2,2,64,128]{6,5,4,3,2,1,0:T(8,128)} custom-call(s32[5]{0:T(128)S(1)} %stack.23.pos, f32[2,4,2,64,128]{4,3,2,1,0:T(8,128)S(1)} %bitcast.36, f32[2,4,2,64,128]{4,3,2,1,0:T(8,128)S(1)} %collective-permute-done.10.refs_1_, f32[2,4,2,64,128]{4,3,2,1,0:T(8,128)S(1)} %collective-permute-done.11.refs_2_, ...), custom_call_target="tpu_custom_call" | custom-call | tf_op jit(solution)/shard_map/partial_sums/pallas_call | solution.py:117
  208.7 54.7 %reduce-scatter.5.cloned.1.call-done = f32[1,4,2,2,64,128]{5,4,3,2,1,0:T(8,128)} async-done(((f32[8,4,2,2,64,128]{5,4,3,2,1,0:T(8,128)}), f32[1,4,2,2,64,128]{5,4,3,2,1,0:T(8,128)}) %reduce-scatter.5.cloned.1.call-update) | async-done | bytes 524304 | tf_op jit(solution)/shard_map/reduce_scatter | solution.py:157
  263.3 12.8 %all_to_all.22 = f32[4,2,2,64,128]{4,3,2,1,0:T(8,128)S(1)} all-to-all(f32[4,2,2,64,128]{4,3,2,1,0:T(8,128)} %bitcast.44), channel_id=1, replica_groups=mesh['y'=4,'x'=4,'zh'=2,'zl'=4,'c'=2] {'x'}, dimensions={0} | all-to-all | bytes 1048576 | tf_op jit(solution)/shard_map/all_to_all | solution.py:162
  276.1 4.1 %all_to_all.23 = f32[2,8,64,128]{3,2,1,0:T(8,128)S(1)} all-to-all(f32[2,8,64,128]{3,2,1,0:T(8,128)S(1)} %bitcast.40), channel_id=1, replica_groups=mesh['y'=4,'x'=4,'zh'=2,'zl'=4,'c'=2] {'c'}, dimensions={0} | all-to-all | bytes 1048576 | tf_op jit(solution)/shard_map/all_to_all | solution.py:163
  280.2 0.8 copy.11
  (29 shorter events, 0.5 us)
Async XLA Ops:
  6.5 138.7 %reduce-scatter.3.cloned.1.call-start = ((), (), s32[]{:S(2)}) async-start(), calls=%async_computation.6 | async-start | bytes 4718592 | tf_op jit(solution)/shard_map/reduce_scatter | solution.py:157
  29.8 5.2 %collective-permute-start.6 = (f32[2,4,2,64,128]{4,3,2,1,0:T(8,128)S(1)}, f32[2,4,2,64,128]{4,3,2,1,0:T(8,128)S(1)}, u32[]{:S(2)}, u32[]{:S(2)}) collective-permute-start(f32[2,4,2,64,128]{4,3,2,1,0:T(8,128)S(1)} %bitcast.20), channel_id=1, source_target_pairs={{0,1},{1,0},{2,3},{3,2},{4,5},{5,4},{6,7},{7,6},{8,9},{9,8},{10,11... | collective-permute-start | bytes 1572872 | tf_op jit(solution)/shard_map/ppermute | solution.py:154
  29.8 26.1 %collective-permute-start.5 = (f32[2,4,2,64,128]{4,3,2,1,0:T(8,128)S(1)}, f32[2,4,2,64,128]{4,3,2,1,0:T(8,128)S(1)}, u32[]{:S(2)}, u32[]{:S(2)}) collective-permute-start(f32[2,4,2,64,128]{4,3,2,1,0:T(8,128)S(1)} %bitcast.21), channel_id=1, source_target_pairs={{0,192},{64,0},{128,64},{192,128},{1,193},{65,1},{129,65},{193,129... | collective-permute-start | bytes 1572872 | tf_op jit(solution)/shard_map/ppermute | solution.py:153
  32.8 24.6 %collective-permute-start.4 = (f32[2,4,2,64,128]{4,3,2,1,0:T(8,128)S(1)}, f32[2,4,2,64,128]{4,3,2,1,0:T(8,128)S(1)}, u32[]{:S(2)}, u32[]{:S(2)}) collective-permute-start(f32[2,4,2,64,128]{4,3,2,1,0:T(8,128)S(1)} %bitcast.22), channel_id=1, source_target_pairs={{0,128},{64,192},{128,0},{192,64},{1,129},{65,193},{129,1},{193,65... | collective-permute-start | bytes 1572872 | tf_op jit(solution)/shard_map/ppermute | solution.py:153
  33.4 26.2 %collective-permute-start.3 = (f32[2,4,2,64,128]{4,3,2,1,0:T(8,128)S(1)}, f32[2,4,2,64,128]{4,3,2,1,0:T(8,128)S(1)}, u32[]{:S(2)}, u32[]{:S(2)}) collective-permute-start(f32[2,4,2,64,128]{4,3,2,1,0:T(8,128)S(1)} %bitcast.23), channel_id=1, source_target_pairs={{0,64},{64,128},{128,192},{192,0},{1,65},{65,129},{129,193},{193,1... | collective-permute-start | bytes 1572872 | tf_op jit(solution)/shard_map/ppermute | solution.py:153
  34.4 25.2 %collective-permute-start.2 = (f32[2,4,2,64,128]{4,3,2,1,0:T(8,128)S(1)}, f32[2,4,2,64,128]{4,3,2,1,0:T(8,128)S(1)}, u32[]{:S(2)}, u32[]{:S(2)}) collective-permute-start(f32[2,4,2,64,128]{4,3,2,1,0:T(8,128)S(1)} %bitcast.24), channel_id=1, source_target_pairs={{0,48},{16,0},{32,16},{48,32},{1,49},{17,1},{33,17},{49,33},{2,50}... | collective-permute-start | bytes 1572872 | tf_op jit(solution)/shard_map/ppermute | solution.py:152
  34.9 25.3 %collective-permute-start.1 = (f32[2,4,2,64,128]{4,3,2,1,0:T(8,128)S(1)}, f32[2,4,2,64,128]{4,3,2,1,0:T(8,128)}, u32[]{:S(2)}, u32[]{:S(2)}) collective-permute-start(f32[2,4,2,64,128]{4,3,2,1,0:T(8,128)S(1)} %bitcast.25), channel_id=1, source_target_pairs={{0,32},{16,48},{32,0},{48,16},{1,33},{17,49},{33,1},{49,17},{2,34}... | collective-permute-start | bytes 1572872 | tf_op jit(solution)/shard_map/ppermute | solution.py:152
  55.9 13.4 %collective-permute-start = (f32[2,4,2,64,128]{4,3,2,1,0:T(8,128)S(1)}, f32[2,4,2,64,128]{4,3,2,1,0:T(8,128)}, u32[]{:S(2)}, u32[]{:S(2)}) collective-permute-start(f32[2,4,2,64,128]{4,3,2,1,0:T(8,128)S(1)} %bitcast.26), channel_id=1, source_target_pairs={{0,16},{16,32},{32,48},{48,0},{1,17},{17,33},{33,49},{49,1},{2,18}... | collective-permute-start | bytes 1572872 | tf_op jit(solution)/shard_map/ppermute | solution.py:152
  57.4 11.9 %collective-permute-start.9 = (f32[2,4,2,64,128]{4,3,2,1,0:T(8,128)S(1)}, f32[2,4,2,64,128]{4,3,2,1,0:T(8,128)}, u32[]{:S(2)}, u32[]{:S(2)}) collective-permute-start(f32[2,4,2,64,128]{4,3,2,1,0:T(8,128)S(1)} %collective-permute-done.5.refs_7_), channel_id=1, source_target_pairs={{0,1},{1,0},{2,3},{3,2},{4,5},{5,4},{6,7},{7,6},{8,9},{9,8},{10,11... | collective-permute-start | bytes 1572872 | tf_op jit(solution)/shard_map/ppermute | solution.py:154
  59.6 9.7 %collective-permute-start.8 = (f32[2,4,2,64,128]{4,3,2,1,0:T(8,128)S(1)}, f32[2,4,2,64,128]{4,3,2,1,0:T(8,128)}, u32[]{:S(2)}, u32[]{:S(2)}) collective-permute-start(f32[2,4,2,64,128]{4,3,2,1,0:T(8,128)S(1)} %collective-permute-done.4.refs_6_), channel_id=1, source_target_pairs={{0,1},{1,0},{2,3},{3,2},{4,5},{5,4},{6,7},{7,6},{8,9},{9,8},{10,11... | collective-permute-start | bytes 1572872 | tf_op jit(solution)/shard_map/ppermute | solution.py:154
  59.6 9.7 %collective-permute-start.7 = (f32[2,4,2,64,128]{4,3,2,1,0:T(8,128)S(1)}, f32[2,4,2,64,128]{4,3,2,1,0:T(8,128)}, u32[]{:S(2)}, u32[]{:S(2)}) collective-permute-start(f32[2,4,2,64,128]{4,3,2,1,0:T(8,128)S(1)} %collective-permute-done.3.refs_5_), channel_id=1, source_target_pairs={{0,1},{1,0},{2,3},{3,2},{4,5},{5,4},{6,7},{7,6},{8,9},{9,8},{10,11... | collective-permute-start | bytes 1572872 | tf_op jit(solution)/shard_map/ppermute | solution.py:154
  69.3 0.8 copy-start
  87.4 110.0 %copy-start.1 = (f32[64,128]{1,0:T(8,128)S(1)}, f32[64,128]{1,0:T(8,128)}, u32[]{:S(2)}) copy-start(f32[64,128]{1,0:T(8,128)} %refs_12_.3) | copy-start | bytes 98308
  87.5 175.8 %reduce-scatter.5.cloned.1.call-start = ((), (), s32[]{:S(2)}) async-start(), calls=%async_computation.7 | async-start | bytes 4718592 | tf_op jit(solution)/shard_map/reduce_scatter | solution.py:157
  158.0 6.3 %collective-permute-start.16 = (f32[2,4,2,64,128]{4,3,2,1,0:T(8,128)S(1)}, f32[2,4,2,64,128]{4,3,2,1,0:T(8,128)S(1)}, u32[]{:S(2)}, u32[]{:S(2)}) collective-permute-start(f32[2,4,2,64,128]{4,3,2,1,0:T(8,128)S(1)} %bitcast.29), channel_id=1, source_target_pairs={{0,1},{1,0},{2,3},{3,2},{4,5},{5,4},{6,7},{7,6},{8,9},{9,8},{10,11... | collective-permute-start | bytes 1572872 | tf_op jit(solution)/shard_map/ppermute | solution.py:154
  158.3 25.9 %collective-permute-start.15 = (f32[2,4,2,64,128]{4,3,2,1,0:T(8,128)S(1)}, f32[2,4,2,64,128]{4,3,2,1,0:T(8,128)S(1)}, u32[]{:S(2)}, u32[]{:S(2)}) collective-permute-start(f32[2,4,2,64,128]{4,3,2,1,0:T(8,128)S(1)} %bitcast.30), channel_id=1, source_target_pairs={{0,192},{64,0},{128,64},{192,128},{1,193},{65,1},{129,65},{193,129... | collective-permute-start | bytes 1572872 | tf_op jit(solution)/shard_map/ppermute | solution.py:153
  161.1 23.3 %collective-permute-start.14 = (f32[2,4,2,64,128]{4,3,2,1,0:T(8,128)S(1)}, f32[2,4,2,64,128]{4,3,2,1,0:T(8,128)S(1)}, u32[]{:S(2)}, u32[]{:S(2)}) collective-permute-start(f32[2,4,2,64,128]{4,3,2,1,0:T(8,128)S(1)} %bitcast.31), channel_id=1, source_target_pairs={{0,128},{64,192},{128,0},{192,64},{1,129},{65,193},{129,1},{193,65... | collective-permute-start | bytes 1572872 | tf_op jit(solution)/shard_map/ppermute | solution.py:153
  162.0 25.9 %collective-permute-start.13 = (f32[2,4,2,64,128]{4,3,2,1,0:T(8,128)S(1)}, f32[2,4,2,64,128]{4,3,2,1,0:T(8,128)S(1)}, u32[]{:S(2)}, u32[]{:S(2)}) collective-permute-start(f32[2,4,2,64,128]{4,3,2,1,0:T(8,128)S(1)} %bitcast.32), channel_id=1, source_target_pairs={{0,64},{64,128},{128,192},{192,0},{1,65},{65,129},{129,193},{193,1... | collective-permute-start | bytes 1572872 | tf_op jit(solution)/shard_map/ppermute | solution.py:153
  162.8 25.0 %collective-permute-start.12 = (f32[2,4,2,64,128]{4,3,2,1,0:T(8,128)S(1)}, f32[2,4,2,64,128]{4,3,2,1,0:T(8,128)S(1)}, u32[]{:S(2)}, u32[]{:S(2)}) collective-permute-start(f32[2,4,2,64,128]{4,3,2,1,0:T(8,128)S(1)} %bitcast.33), channel_id=1, source_target_pairs={{0,48},{16,0},{32,16},{48,32},{1,49},{17,1},{33,17},{49,33},{2,50}... | collective-permute-start | bytes 1572872 | tf_op jit(solution)/shard_map/ppermute | solution.py:152
  164.3 24.1 %collective-permute-start.11 = (f32[2,4,2,64,128]{4,3,2,1,0:T(8,128)S(1)}, f32[2,4,2,64,128]{4,3,2,1,0:T(8,128)S(1)}, u32[]{:S(2)}, u32[]{:S(2)}) collective-permute-start(f32[2,4,2,64,128]{4,3,2,1,0:T(8,128)S(1)} %bitcast.34), channel_id=1, source_target_pairs={{0,32},{16,48},{32,0},{48,16},{1,33},{17,49},{33,1},{49,17},{2,34}... | collective-permute-start | bytes 1572872 | tf_op jit(solution)/shard_map/ppermute | solution.py:152
  184.2 13.2 %collective-permute-start.10 = (f32[2,4,2,64,128]{4,3,2,1,0:T(8,128)S(1)}, f32[2,4,2,64,128]{4,3,2,1,0:T(8,128)S(1)}, u32[]{:S(2)}, u32[]{:S(2)}) collective-permute-start(f32[2,4,2,64,128]{4,3,2,1,0:T(8,128)S(1)} %bitcast.35), channel_id=1, source_target_pairs={{0,16},{16,32},{32,48},{48,0},{1,17},{17,33},{33,49},{49,1},{2,18}... | collective-permute-start | bytes 1572872 | tf_op jit(solution)/shard_map/ppermute | solution.py:152
  184.4 13.0 %collective-permute-start.19 = (f32[2,4,2,64,128]{4,3,2,1,0:T(8,128)S(1)}, f32[2,4,2,64,128]{4,3,2,1,0:T(8,128)S(1)}, u32[]{:S(2)}, u32[]{:S(2)}) collective-permute-start(f32[2,4,2,64,128]{4,3,2,1,0:T(8,128)S(1)} %collective-permute-done.15.refs_7_), channel_id=1, source_target_pairs={{0,1},{1,0},{2,3},{3,2},{4,5},{5,4},{6,7},{7,6},{8,9},{9,8},{10,11... | collective-permute-start | bytes 1572872 | tf_op jit(solution)/shard_map/ppermute | solution.py:154
  187.8 9.5 %collective-permute-start.18 = (f32[2,4,2,64,128]{4,3,2,1,0:T(8,128)S(1)}, f32[2,4,2,64,128]{4,3,2,1,0:T(8,128)S(1)}, u32[]{:S(2)}, u32[]{:S(2)}) collective-permute-start(f32[2,4,2,64,128]{4,3,2,1,0:T(8,128)S(1)} %collective-permute-done.14.refs_6_), channel_id=1, source_target_pairs={{0,1},{1,0},{2,3},{3,2},{4,5},{5,4},{6,7},{7,6},{8,9},{9,8},{10,11... | collective-permute-start | bytes 1572872 | tf_op jit(solution)/shard_map/ppermute | solution.py:154
  187.9 9.5 %collective-permute-start.17 = (f32[2,4,2,64,128]{4,3,2,1,0:T(8,128)S(1)}, f32[2,4,2,64,128]{4,3,2,1,0:T(8,128)S(1)}, u32[]{:S(2)}, u32[]{:S(2)}) collective-permute-start(f32[2,4,2,64,128]{4,3,2,1,0:T(8,128)S(1)} %collective-permute-done.13.refs_5_), channel_id=1, source_target_pairs={{0,1},{1,0},{2,3},{3,2},{4,5},{5,4},{6,7},{7,6},{8,9},{9,8},{10,11... | collective-permute-start | bytes 1572872 | tf_op jit(solution)/shard_map/ppermute | solution.py:154
Sparse Core Ops, SparseCore 0:
  87.6 57.6 reduce-scatter.2
  208.8 54.4 reduce-scatter.4
